TPU v7x, 32 devices: a whole 2x2x4 slice. The times are simulated.
32 devices in a mesh: node: 16 (over z, y, x), rep: 2 (over core).
Axes of the slice: x: 2, y: 2, z: 4, core: 2. Of those that a mesh axis runs over, the one named last changes fastest.
Arguments:
- features: bfloat16 [4096, 512], P(('rep', 'node')), parts along dimension 0, may hold values from -24 to 24
- upstream: bfloat16 [4096, 512], P(('rep', 'node')), parts along dimension 0, may hold values from -36 to 36
- weight_one: bfloat16 [512, 512], replicated, may hold values from -0.25 to 0.25
- weight_two: bfloat16 [512, 512], replicated, may hold values from -0.25 to 0.25
- neighbours: int32 [4096, 32], P(('rep', 'node')), parts along dimension 0, may hold values from 0 to 2047, as said below
- edge_weight: int32 [4096, 32], P(('rep', 'node')), parts along dimension 0, may hold values from 1 to 8
- fetch_block: int32 [512, 2], P('rep'), parts along dimension 0, may hold values from 0 to 15, as said below
- fetch_count: int32 [512], P('rep'), parts along dimension 0, may hold values from 0 to 2, as said below
Outputs:
- d_features: bfloat16 [4096, 512], P(('rep', 'node')), parts along dimension 0
- grad_one: bfloat16 [1024, 512], P('rep'), parts along dimension 0
- grad_two: bfloat16 [1024, 512], P('rep'), parts along dimension 0
There are 2 independent parts, one for each index of `rep`. A program takes and returns all parts, laid end to end along the dimension named above; an argument that names none is the same for every part. Nothing has to cross between parts.
Inputs may be any that keep to these rules, and one draw needn't show every extreme that they name: `neighbours`: no node names itself. `fetch_block`: the 2 blocks listed for one pair of devices are distinct. `fetch_count`: zero where p = d; every device has 2 live blocks from some other device.
All inputs are finite; a program needn't handle non-finite values.
Results may differ from a plain program's by a relative error of at most 0.013.
Values may be sent and summed in bfloat16 or wider, within the bound.
No kernel may reach another device: no remote copies, remote signals or barrier semaphores. Data moves between devices by JAX's collectives and lax.ppermute only.
A program may use at most 64 MiB of HBM per device.

v0:
```python
import math
import jax
import jax.numpy as jnp
from jax import lax
from jax.sharding import PartitionSpec as P

D = 512
ROWS = 128
HALO = 32
BLK = 8
CAP = 2
SELF_WEIGHT = 8.0


def with_halo(block, sides, width):
    for axis, dim in sides:
        count = lax.axis_size(axis)
        forward = [(i, i + 1) for i in range(count - 1)]
        backward = [(target, source) for source, target in forward]
        low = lax.ppermute(
            lax.slice_in_dim(block, block.shape[dim] - width, None, axis=dim), axis, forward
        )
        high = lax.ppermute(lax.slice_in_dim(block, 0, width, axis=dim), axis, backward)
        block = jnp.concatenate([low, block, high], axis=dim)
    return block


def gelu_tanh(values):
    return jax.nn.gelu(values, approximate=True)


def edge_tables(neighbours, edge_weight, fetch_block, fetch_count, peer_count, device):
    first_row = device * ROWS
    local_rows = jnp.arange(ROWS, dtype=jnp.int32)
    owner_dev = neighbours // ROWS
    in_band = (neighbours >= first_row - HALO) & (neighbours < first_row + ROWS + HALO)
    my_table = lax.dynamic_slice_in_dim(fetch_block, device * peer_count, peer_count, 0)
    my_counts = lax.dynamic_slice_in_dim(fetch_count, device * peer_count, peer_count, 0)
    target = neighbours % ROWS // BLK
    listed = jnp.take(my_table, owner_dev, axis=0)
    live_slot = (
        jnp.arange(CAP, dtype=jnp.int32)[None, None, :] < jnp.take(my_counts, owner_dev)[..., None]
    )
    matched = (listed == target[..., None]) & live_slot
    found_slot = jnp.any(matched, axis=-1)
    slot_index = jnp.argmax(matched, axis=-1)
    weight = edge_weight.astype(jnp.float32)
    band_weight = jnp.where(in_band, weight, 0.0)
    far_use = jnp.logical_not(in_band) & found_slot
    far_weight = jnp.where(far_use, weight, 0.0)
    band_col = jnp.where(in_band, neighbours - first_row + HALO, 0)
    far_col = jnp.where(far_use, (owner_dev * CAP + slot_index) * BLK + neighbours % BLK, 0)
    row_index = jnp.broadcast_to(local_rows[:, None], neighbours.shape)
    band_matrix = (
        jnp.zeros((ROWS, ROWS + 2 * HALO), jnp.float32).at[row_index, band_col].add(band_weight)
    )
    band_matrix = band_matrix.at[local_rows, local_rows + HALO].add(SELF_WEIGHT)
    far_matrix = (
        jnp.zeros((ROWS, peer_count * CAP * BLK), jnp.float32)
        .at[row_index, far_col]
        .add(far_weight)
    )
    row_total = SELF_WEIGHT + jnp.sum(band_weight + far_weight, axis=1)
    asked_blocks = jnp.take(
        fetch_block, jnp.arange(peer_count, dtype=jnp.int32) * peer_count + device, axis=0
    )
    return (
        band_matrix.astype(jnp.bfloat16),
        far_matrix.astype(jnp.bfloat16),
        row_total,
        asked_blocks,
    )


def aggregate(values, band_matrix, far_matrix, row_total, asked_blocks):
    extended = with_halo(values, (("node", 0),), HALO)
    outgoing = values.reshape(ROWS // BLK, BLK, D)[asked_blocks]
    incoming = lax.all_to_all(outgoing, "node", split_axis=0, concat_axis=0, tiled=True)
    sums = jnp.dot(band_matrix, extended, preferred_element_type=jnp.float32)
    sums = sums + jnp.dot(far_matrix, incoming.reshape(-1, D), preferred_element_type=jnp.float32)
    return (sums / row_total[:, None]).astype(jnp.bfloat16)


def adjoint(cotangent, band_matrix, far_matrix, asked_blocks, peer_count):
    back_band = lax.dot_general(
        band_matrix, cotangent, (((0,), (0,)), ((), ())), preferred_element_type=jnp.float32
    )
    own_rows = back_band[HALO : HALO + ROWS]
    rim_terms = jnp.concatenate([back_band[:HALO], back_band[HALO + ROWS :]], axis=0)
    rim_back = with_halo(rim_terms.astype(jnp.bfloat16), (("node", 0),), HALO).astype(
        rim_terms.dtype
    )
    own_rows = own_rows.at[:HALO].add(rim_back[:HALO])
    own_rows = own_rows.at[ROWS - HALO :].add(rim_back[3 * HALO :])
    back_far = lax.dot_general(
        far_matrix, cotangent, (((0,), (0,)), ((), ())), preferred_element_type=jnp.float32
    )
    back_far = back_far.reshape(peer_count, CAP, BLK, D)
    returned = lax.all_to_all(
        back_far.astype(jnp.bfloat16), "node", split_axis=0, concat_axis=0, tiled=True
    ).astype(back_far.dtype)
    own_rows = own_rows.reshape(ROWS // BLK, BLK, D).at[asked_blocks].add(returned)
    return own_rows.reshape(ROWS, D)


def contract_rows(left, right):
    return lax.dot_general(
        left, right, (((0,), (0,)), ((), ())), preferred_element_type=jnp.float32
    )


def sum_weight_grad(partial_grad):
    return lax.psum(partial_grad, "node")


def shards(
    features, upstream, weight_one, weight_two, neighbours, edge_weight, fetch_block, fetch_count
):
    peer_count = lax.axis_size("node")
    device = lax.axis_index("node")
    band_matrix, far_matrix, row_total, asked_blocks = edge_tables(
        neighbours, edge_weight, fetch_block, fetch_count, peer_count, device
    )
    grad_scale = 1.0 / math.sqrt(ROWS * peer_count)
    agg_one = aggregate(features, band_matrix, far_matrix, row_total, asked_blocks)
    pre_one = jnp.dot(agg_one, weight_one, preferred_element_type=jnp.float32)
    hidden_f, gelu_back = jax.vjp(gelu_tanh, pre_one)
    hidden = hidden_f.astype(jnp.bfloat16)
    agg_two = aggregate(hidden, band_matrix, far_matrix, row_total, asked_blocks)
    part_two = contract_rows(agg_two, upstream)
    summed_two = sum_weight_grad(part_two)
    q_two = lax.dot_general(
        upstream, weight_two, (((1,), (1,)), ((), ())), preferred_element_type=jnp.float32
    )
    q_two = (q_two / row_total[:, None]).astype(jnp.bfloat16)
    back_hidden = adjoint(q_two, band_matrix, far_matrix, asked_blocks, peer_count)
    d_pre = gelu_back(back_hidden)[0].astype(jnp.bfloat16)
    part_one = contract_rows(agg_one, d_pre)
    summed_one = sum_weight_grad(part_one)
    q_one = lax.dot_general(
        d_pre, weight_one, (((1,), (1,)), ((), ())), preferred_element_type=jnp.float32
    )
    q_one = (q_one / row_total[:, None]).astype(jnp.bfloat16)
    d_features = adjoint(q_one, band_matrix, far_matrix, asked_blocks, peer_count)
    grad_one = (summed_one * grad_scale).astype(jnp.bfloat16)
    grad_two = (summed_two * grad_scale).astype(jnp.bfloat16)
    return (d_features.astype(jnp.bfloat16), grad_one, grad_two)


def solution(mesh):
    placed = (
        P(("rep", "node"), None),
        P(("rep", "node"), None),
        P(),
        P(),
        P(("rep", "node"), None),
        P(("rep", "node"), None),
        P("rep", None),
        P("rep"),
    )
    return jax.shard_map(
        shards,
        mesh=mesh,
        in_specs=placed,
        out_specs=(P(("rep", "node"), None), P("rep", None), P("rep", None)),
        check_vma=False,
    )
```

profile of v0, /device:TPU:0, one launch (start us, length us, event | category | flops | bytes accessed | tf_op | source)
XLA Modules:
  0.0 309.5 jit_solution(4038717599790663979)
XLA Ops:
  7.2 1.5 fusion.62
  8.6 5.4 %collective-permute-start.2 = (bf16[32,512]{1,0:T(8,128)(2,1)}, bf16[32,512]{1,0:T(8,128)(2,1)}, u32[]{:S(2)}, u32[]{:S(2)}) collective-permute-start(bf16[32,512]{1,0:T(8,128)(2,1)} %get-tuple-element.74), channel_id=1, source_target_pairs={{0,2},{2,4},{4,6},{6,8},{8,10},{10,12},{12,14},{14,16},{16,18},{18... | collective-permute-start | bytes 98312 | tf_op jit(solution)/shard_map/ppermute | solution.py:20
  14.1 1.3 collective-permute-start.3
  17.1 2.2 gather_fusion.2
  19.3 8.0 %all-to-all-start.1 = ((bf16[16,2,8,512]{3,2,1,0:T(8,128)(2,1)}), bf16[16,2,8,512]{3,2,1,0:T(8,128)(2,1)S(1)}, u32[]{:S(2)}, u32[]{:S(2)}) async-start(bf16[16,2,8,512]{3,2,1,0:T(8,128)(2,1)} %bitcast.29), calls=%async_computation.1 | async-start | bytes 524288 | tf_op jit(solution)/shard_map/all_to_all | solution.py:78
  30.2 1.3 fusion.45
  31.9 10.1 %select_select_fusion = s32[128,32]{0,1:T(8,128)S(1)} fusion(s32[128,32]{0,1:T(8,128)S(1)} %get-tuple-element.65, s32[]{:T(128)} %bitcast.5, s32[]{:T(128)} %bitcast.6, s32[]{:T(128)} %bitcast.7, s32[]{:T(128)} %bitcast.8, s32[]{:T(128)} %bitcast.9, s32[]{:T(128)} %bitcast.10, s32[]{:T(128)} %bitcast.11, s32[]{:T(128)} %bitcast.12, s32[]{:T(128)} %bitcast.13, ...), kind=kLoop, calls=%fused_computation.100 | loop fusion | flops 139264 | bytes 32832 | tf_op jit(solution)/shard_map/jit(_take)/select_n | solution.py:42
  42.1 10.8 %gather_fusion = s32[4096,2]{1,0:T(8,128)S(1)} fusion(s32[16,2]{1,0:T(8,128)S(1)} %constant_dynamic-slice_fusion, s32[4096]{0:T(1024)S(1)} %broadcast_clamp_fusion), kind=kCustom, calls=%fused_computation | custom fusion | bytes 81920 | tf_op jit(solution)/shard_map/jit(_take)/gather | solution.py:40
  52.8 6.2 %fusion.57 = (pred[128,32]{1,0:T(8,128)(4,1)}, pred[128,32,2]{2,1,0:T(8,128)(4,1)S(1)}) fusion(s32[128,32]{1,0:T(8,128)S(1)} %copy.64, s32[128,32]{1,0:T(8,128)S(1)} %copy.63, s32[128,32,2]{2,1,0:T(8,128)S(1)} %bitcast.88, pred[128,32]{1,0:T(8,128)(4,1)} %copy.60), kind=kLoop, calls=%fused_computation.136 | loop fusion | flops 36864 | bytes 81920 | tf_op jit(solution)/shard_map/reduce_or | solution.py:45
  60.9 5.1 %iota_reduce_fusion = (pred[128,32]{1,0:T(8,128)(4,1)}, s32[128,32]{1,0:T(8,128)S(1)}) fusion(pred[128,32,2]{2,1,0:T(8,128)(4,1)S(1)} %get-tuple-element.63), kind=kLoop, calls=%fused_computation.9 | loop fusion | flops 28672 | bytes 28672 | tf_op jit(solution)/shard_map/edge_tables/reduce | solution.py:46
  68.6 21.9 %scatter_custom_fusion.3 = f32[24576]{0:T(1024)S(1)} fusion(s32[4096]{0:T(1024)S(1)} %reshape.324, f32[4096]{0:T(1024)S(1)} %reshape.326, f32[]{:T(128)} %constant.212.clone.1), kind=kCustom, calls=%fused_computation.67 | custom fusion | flops 4096 | bytes 98308
  90.6 7.1 %scatter_fusion = f32[128,192]{0,1:T(8,128)S(1)} fusion(f32[128,192]{0,1:T(8,128)S(1)} %bitcast.89, s32[128]{0:T(128)S(1)} %fusion.52, f32[128]{0:T(128)S(1)} %broadcast.327), kind=kCustom, calls=%fused_computation.4 | custom fusion | flops 128 | bytes 2560 | tf_op jit(solution)/shard_map/scatter-add | solution.py:57
  98.3 3.8 %collective-permute-start = (bf16[32,512]{1,0:T(8,128)(2,1)S(1)}, bf16[32,512]{1,0:T(8,128)(2,1)S(1)}, u32[]{:S(2)}, u32[]{:S(2)}) collective-permute-start(bf16[32,512]{1,0:T(8,128)(2,1)S(1)} %get-tuple-element.70), channel_id=1, source_target_pairs={{0,2},{2,4},{4,6},{6,8},{8,10},{10,12},{12,14},{14,16},{16,18},{18... | collective-permute-start | bytes 98312 | tf_op jit(solution)/shard_map/ppermute | solution.py:20
  102.1 1.3 collective-permute-start.1
  103.8 28.8 %scatter_custom_fusion.4 = f32[32768]{0:T(1024)S(1)} fusion(s32[4096]{0:T(1024)S(1)} %reshape.330, f32[4096]{0:T(1024)S(1)} %reshape.332, f32[]{:T(128)} %constant.212.clone.1), kind=kCustom, calls=%fused_computation.65 | custom fusion | flops 4096 | bytes 131076
  133.6 7.7 %all-to-all-start = ((bf16[16,2,8,512]{3,2,1,0:T(8,128)(2,1)}), bf16[16,2,8,512]{3,2,1,0:T(8,128)(2,1)S(1)}, u32[]{:S(2)}, u32[]{:S(2)}) async-start(bf16[16,2,8,512]{3,2,1,0:T(8,128)(2,1)} %bitcast.25), calls=%async_computation | async-start | bytes 524288 | tf_op jit(solution)/shard_map/all_to_all | solution.py:99
  142.8 7.0 %all-to-all-done = bf16[16,2,8,512]{3,2,1,0:T(8,128)(2,1)S(1)} async-done(((bf16[16,2,8,512]{3,2,1,0:T(8,128)(2,1)}), bf16[16,2,8,512]{3,2,1,0:T(8,128)(2,1)S(1)}, u32[]{:S(2)}, u32[]{:S(2)}) %all-to-all-start) | async-done | bytes 262176 | tf_op jit(solution)/shard_map/all_to_all | solution.py:99
  149.9 1.9 scatter_fusion.1
  153.2 3.5 %all-to-all-start.3 = ((bf16[16,2,8,512]{3,2,1,0:T(8,128)(2,1)}), bf16[16,2,8,512]{3,2,1,0:T(8,128)(2,1)S(1)}, u32[]{:S(2)}, u32[]{:S(2)}) async-start(bf16[16,2,8,512]{3,2,1,0:T(8,128)(2,1)} %bitcast.36), calls=%async_computation.3 | async-start | bytes 524288 | tf_op jit(solution)/shard_map/all_to_all | solution.py:78
  156.8 3.8 %collective-permute-start.6 = (bf16[32,512]{1,0:T(8,128)(2,1)S(1)}, bf16[32,512]{1,0:T(8,128)(2,1)S(1)}, u32[]{:S(2)}, u32[]{:S(2)}) collective-permute-start(bf16[32,512]{1,0:T(8,128)(2,1)S(1)} %get-tuple-element.72), channel_id=1, source_target_pairs={{0,2},{2,4},{4,6},{6,8},{8,10},{10,12},{12,14},{14,16},{16,18},{18... | collective-permute-start | bytes 98312 | tf_op jit(solution)/shard_map/ppermute | solution.py:20
  160.7 1.3 collective-permute-start.7
  162.0 1.3 fusion.68
  163.3 2.0 all-to-all-done.3
  166.5 1.5 fusion.7
  169.3 7.3 %all-to-all-start.2 = ((bf16[16,2,8,512]{3,2,1,0:T(8,128)(2,1)}), bf16[16,2,8,512]{3,2,1,0:T(8,128)(2,1)S(1)}, u32[]{:S(2)}, u32[]{:S(2)}) async-start(bf16[16,2,8,512]{3,2,1,0:T(8,128)(2,1)} %bitcast.32), calls=%async_computation.2 | async-start | bytes 524288 | tf_op jit(solution)/shard_map/all_to_all | solution.py:99
  176.8 3.8 %collective-permute-start.4 = (bf16[32,512]{1,0:T(8,128)(2,1)S(1)}, bf16[32,512]{1,0:T(8,128)(2,1)S(1)}, u32[]{:S(2)}, u32[]{:S(2)}) collective-permute-start(bf16[32,512]{1,0:T(8,128)(2,1)S(1)} %get-tuple-element.68), channel_id=1, source_target_pairs={{0,2},{2,4},{4,6},{6,8},{8,10},{10,12},{12,14},{14,16},{16,18},{18... | collective-permute-start | bytes 98312 | tf_op jit(solution)/shard_map/ppermute | solution.py:20
  180.7 1.3 collective-permute-start.5
  182.7 3.9 %collective-permute-done.5 = bf16[32,512]{1,0:T(8,128)(2,1)S(1)} collective-permute-done((bf16[32,512]{1,0:T(8,128)(2,1)S(1)}, bf16[32,512]{1,0:T(8,128)(2,1)S(1)}, u32[]{:S(2)}, u32[]{:S(2)}) %collective-permute-start.5) | collective-permute-done | bytes 32800 | tf_op jit(solution)/shard_map/ppermute | solution.py:23
  186.7 2.6 all-to-all-done.2
  189.4 1.9 scatter_fusion.2
  191.9 107.6 %all-reduce.3.cloned.1.call-done = (f32[512,512]{1,0:T(8,128)}, f32[512,512]{1,0:T(8,128)}) async-done(((f32[512,512]{1,0:T(8,128)}, f32[512,512]{1,0:T(8,128)}), (f32[512,512]{1,0:T(8,128)}, f32[512,512]{1,0:T(8,128)})) %all-reduce.3.cloned.1.call-update) | async-done | bytes 2097168 | tf_op jit(solution)/shard_map/psum | solution.py:113
  299.5 2.2 multiply_convert_fusion.1
  (91 shorter events, 19.5 us)
Async XLA Ops:
  7.2 135.4 %copy-start = (bf16[512,512]{1,0:T(8,128)(2,1)S(1)}, bf16[512,512]{1,0:T(8,128)(2,1)}, u32[]{:S(2)}) copy-start(bf16[512,512]{1,0:T(8,128)(2,1)} %param.18) | copy-start | bytes 1572868
  8.6 132.9 %collective-permute-start.2 = (bf16[32,512]{1,0:T(8,128)(2,1)}, bf16[32,512]{1,0:T(8,128)(2,1)}, u32[]{:S(2)}, u32[]{:S(2)}) collective-permute-start(bf16[32,512]{1,0:T(8,128)(2,1)} %get-tuple-element.74), channel_id=1, source_target_pairs={{0,2},{2,4},{4,6},{6,8},{8,10},{10,12},{12,14},{14,16},{16,18},{18... | collective-permute-start | bytes 98312 | tf_op jit(solution)/shard_map/ppermute | solution.py:20
  14.1 127.5 %collective-permute-start.3 = (bf16[32,512]{1,0:T(8,128)(2,1)}, bf16[32,512]{1,0:T(8,128)(2,1)}, u32[]{:S(2)}, u32[]{:S(2)}) collective-permute-start(bf16[32,512]{1,0:T(8,128)(2,1)} %get-tuple-element.75), channel_id=1, source_target_pairs={{2,0},{4,2},{6,4},{8,6},{10,8},{12,10},{14,12},{16,14},{18,16},{20... | collective-permute-start | bytes 98312 | tf_op jit(solution)/shard_map/ppermute | solution.py:23
  17.1 10.2 %copy-start.4 = (s32[1024]{0:T(1024)}, s32[1024]{0:T(1024)S(1)}, u32[]{:S(2)}) copy-start(s32[1024]{0:T(1024)S(1)} %pad_clamp_fusion) | copy-start | bytes 12292
  19.3 114.4 %all-to-all-start.1 = ((bf16[16,2,8,512]{3,2,1,0:T(8,128)(2,1)}), bf16[16,2,8,512]{3,2,1,0:T(8,128)(2,1)S(1)}, u32[]{:S(2)}, u32[]{:S(2)}) async-start(bf16[16,2,8,512]{3,2,1,0:T(8,128)(2,1)} %bitcast.29), calls=%async_computation.1 | async-start | bytes 524288 | tf_op jit(solution)/shard_map/all_to_all | solution.py:78
  59.0 38.7 %copy-start.3 = (bf16[128,512]{1,0:T(8,128)(2,1)S(1)}, bf16[128,512]{1,0:T(8,128)(2,1)}, u32[]{:S(2)}) copy-start(bf16[128,512]{1,0:T(8,128)(2,1)} %param.17) | copy-start | bytes 393220
  59.0 38.7 %copy-start.6 = (bf16[512,512]{1,0:T(8,128)(2,1)S(1)}, bf16[512,512]{1,0:T(8,128)(2,1)}, u32[]{:S(2)}) copy-start(bf16[512,512]{1,0:T(8,128)(2,1)} %param.19) | copy-start | bytes 1572868
  98.1 43.5 %copy-start.2 = (bf16[128,512]{1,0:T(8,128)(2,1)S(1)}, bf16[128,512]{1,0:T(8,128)(2,1)}, u32[]{:S(2)}) copy-start(bf16[128,512]{1,0:T(8,128)(2,1)} %param.16) | copy-start | bytes 393220
  98.3 35.3 %collective-permute-start = (bf16[32,512]{1,0:T(8,128)(2,1)S(1)}, bf16[32,512]{1,0:T(8,128)(2,1)S(1)}, u32[]{:S(2)}, u32[]{:S(2)}) collective-permute-start(bf16[32,512]{1,0:T(8,128)(2,1)S(1)} %get-tuple-element.70), channel_id=1, source_target_pairs={{0,2},{2,4},{4,6},{6,8},{8,10},{10,12},{12,14},{14,16},{16,18},{18... | collective-permute-start | bytes 98312 | tf_op jit(solution)/shard_map/ppermute | solution.py:20
  102.1 31.5 %collective-permute-start.1 = (bf16[32,512]{1,0:T(8,128)(2,1)S(1)}, bf16[32,512]{1,0:T(8,128)(2,1)S(1)}, u32[]{:S(2)}, u32[]{:S(2)}) collective-permute-start(bf16[32,512]{1,0:T(8,128)(2,1)S(1)} %get-tuple-element.71), channel_id=1, source_target_pairs={{2,0},{4,2},{6,4},{8,6},{10,8},{12,10},{14,12},{16,14},{18,16},{20... | collective-permute-start | bytes 98312 | tf_op jit(solution)/shard_map/ppermute | solution.py:23
  133.6 16.2 %all-to-all-start = ((bf16[16,2,8,512]{3,2,1,0:T(8,128)(2,1)}), bf16[16,2,8,512]{3,2,1,0:T(8,128)(2,1)S(1)}, u32[]{:S(2)}, u32[]{:S(2)}) async-start(bf16[16,2,8,512]{3,2,1,0:T(8,128)(2,1)} %bitcast.25), calls=%async_computation | async-start | bytes 524288 | tf_op jit(solution)/shard_map/all_to_all | solution.py:99
  142.5 9.4 %copy-start.5 = (s32[1024]{0:T(1024)S(1)}, s32[1024]{0:T(1024)}, u32[]{:S(2)}) copy-start(s32[1024]{0:T(1024)} %copy-done.4) | copy-start | bytes 12292
  153.2 12.0 %all-to-all-start.3 = ((bf16[16,2,8,512]{3,2,1,0:T(8,128)(2,1)}), bf16[16,2,8,512]{3,2,1,0:T(8,128)(2,1)S(1)}, u32[]{:S(2)}, u32[]{:S(2)}) async-start(bf16[16,2,8,512]{3,2,1,0:T(8,128)(2,1)} %bitcast.36), calls=%async_computation.3 | async-start | bytes 524288 | tf_op jit(solution)/shard_map/all_to_all | solution.py:78
  156.8 142.7 %all-reduce.3.cloned.1.call-start = ((), (), s32[]{:S(2)}) async-start(), calls=%async_computation.4 | async-start | bytes 4194304 | tf_op jit(solution)/shard_map/psum | solution.py:113
  156.8 8.6 %collective-permute-start.6 = (bf16[32,512]{1,0:T(8,128)(2,1)S(1)}, bf16[32,512]{1,0:T(8,128)(2,1)S(1)}, u32[]{:S(2)}, u32[]{:S(2)}) collective-permute-start(bf16[32,512]{1,0:T(8,128)(2,1)S(1)} %get-tuple-element.72), channel_id=1, source_target_pairs={{0,2},{2,4},{4,6},{6,8},{8,10},{10,12},{12,14},{14,16},{16,18},{18... | collective-permute-start | bytes 98312 | tf_op jit(solution)/shard_map/ppermute | solution.py:20
  160.7 5.8 %collective-permute-start.7 = (bf16[32,512]{1,0:T(8,128)(2,1)S(1)}, bf16[32,512]{1,0:T(8,128)(2,1)S(1)}, u32[]{:S(2)}, u32[]{:S(2)}) collective-permute-start(bf16[32,512]{1,0:T(8,128)(2,1)S(1)} %get-tuple-element.73), channel_id=1, source_target_pairs={{2,0},{4,2},{6,4},{8,6},{10,8},{12,10},{14,12},{16,14},{18,16},{20... | collective-permute-start | bytes 98312 | tf_op jit(solution)/shard_map/ppermute | solution.py:23
  169.3 20.0 %all-to-all-start.2 = ((bf16[16,2,8,512]{3,2,1,0:T(8,128)(2,1)}), bf16[16,2,8,512]{3,2,1,0:T(8,128)(2,1)S(1)}, u32[]{:S(2)}, u32[]{:S(2)}) async-start(bf16[16,2,8,512]{3,2,1,0:T(8,128)(2,1)} %bitcast.32), calls=%async_computation.2 | async-start | bytes 524288 | tf_op jit(solution)/shard_map/all_to_all | solution.py:99
  176.8 5.9 %collective-permute-start.4 = (bf16[32,512]{1,0:T(8,128)(2,1)S(1)}, bf16[32,512]{1,0:T(8,128)(2,1)S(1)}, u32[]{:S(2)}, u32[]{:S(2)}) collective-permute-start(bf16[32,512]{1,0:T(8,128)(2,1)S(1)} %get-tuple-element.68), channel_id=1, source_target_pairs={{0,2},{2,4},{4,6},{6,8},{8,10},{10,12},{12,14},{14,16},{16,18},{18... | collective-permute-start | bytes 98312 | tf_op jit(solution)/shard_map/ppermute | solution.py:20
  180.7 6.0 %collective-permute-start.5 = (bf16[32,512]{1,0:T(8,128)(2,1)S(1)}, bf16[32,512]{1,0:T(8,128)(2,1)S(1)}, u32[]{:S(2)}, u32[]{:S(2)}) collective-permute-start(bf16[32,512]{1,0:T(8,128)(2,1)S(1)} %get-tuple-element.69), channel_id=1, source_target_pairs={{2,0},{4,2},{6,4},{8,6},{10,8},{12,10},{14,12},{16,14},{18,16},{20... | collective-permute-start | bytes 98312 | tf_op jit(solution)/shard_map/ppermute | solution.py:23
  299.5 2.2 copy-start.1
Sparse Core Ops, SparseCore 0:
  168.1 131.2 all-reduce.2
where the time goes:
time: 311 us; the launch traced here: 309 us
  waiting for transfers between devices  125 us (40%)
  other arithmetic  92.5 us (30%)
  starting transfers between devices  48.7 us (16%)
  local copies, waits for them, and re-layouts  21.6 us (7%)
  between operations  14.6 us (5%)
  matrix products  7.27 us (2%)
    psum x1, waiting for transfers between devices, sum_weight_grad(): return lax.psum(partial_grad, 'node')  108 us
    unnamed x5, other arithmetic  52.4 us
    ppermute x4, starting transfers between devices, with_halo(): lax.ppermute(lax.slice_in_dim(block, block.shape[dim] - width, None, axis...  16.9 us
    all_to_all x2, starting transfers between devices, adjoint(): lax.all_to_all(back_far.astype(jnp.bfloat16), 'node', split_axis=0, conca...  15 us
    all_to_all x2, starting transfers between devices, aggregate(): lax.all_to_all(outgoing, 'node', split_axis=0, concat_axis=0, tiled=True)  11.6 us
    gather x1, local copies, waits for them, and re-layouts, edge_tables(): listed = jnp.take(my_table, owner_dev, axis=0)  10.8 us
    select_n x1, other arithmetic, edge_tables(): jnp.take(my_counts, owner_dev)[..., None]  10.1 us
    all_to_all x2, waiting for transfers between devices, adjoint(): lax.all_to_all(back_far.astype(jnp.bfloat16), 'node', split_axis=0, conca...  9.64 us
  transfers between devices with their start and end apart: 13, of which 7 were waited for; matrix products, arithmetic and copies ran while one was open for 36% of the time, Pallas kernels for 0%

commit v1 on v0

--- a/solution.py
+++ b/solution.py
@@ -110,7 +110,7 @@
 
 
 def sum_weight_grad(partial_grad):
-    return lax.psum(partial_grad, "node")
+    return jnp.sum(lax.all_gather(partial_grad, "node"), axis=0)
 
 
 def shards(

time: 311 us -> 560 us (1.80)
  waiting for transfers between devices: 125 us -> 359 us
  other arithmetic: 92.5 us -> 107 us
    all_gather x0 -> x2, waiting for transfers between devices: none -> 340 us  [sum_weight_grad(): return jnp.sum(lax.all_gather(partial_grad, 'node'), axis=0)]
    psum x1 -> x0, waiting for transfers between devices: 108 us -> none  [sum_weight_grad(): return lax.psum(partial_grad, 'node')]
    reduce_sum x0 -> x2, other arithmetic: none -> 15.8 us  [sum_weight_grad(): return jnp.sum(lax.all_gather(partial_grad, 'node'), axis=0)]
  transfers between devices with their start and end apart: 13 -> 14, of which waited for: 7 -> 8; matrix products, arithmetic and copies ran while one was open for 36% -> 22% of each run, Pallas kernels for 0% -> 0%
where the time goes in v1:
time: 560 us; the launch traced here: 559 us
  waiting for transfers between devices  359 us (64%)
  other arithmetic  107 us (19%)
  starting transfers between devices  49 us (9%)
  local copies, waits for them, and re-layouts  21.6 us (4%)
  between operations  14.6 us (3%)
  matrix products  7.3 us (1%)
    all_gather x2, waiting for transfers between devices, sum_weight_grad(): return jnp.sum(lax.all_gather(partial_grad, 'node'), axis=0)  340 us
    unnamed x5, other arithmetic  52.4 us
    ppermute x4, starting transfers between devices, with_halo(): lax.ppermute(lax.slice_in_dim(block, block.shape[dim] - width, None, axis...  16.9 us
    reduce_sum x2, other arithmetic, sum_weight_grad(): return jnp.sum(lax.all_gather(partial_grad, 'node'), axis=0)  15.8 us
    all_to_all x2, starting transfers between devices, adjoint(): lax.all_to_all(back_far.astype(jnp.bfloat16), 'node', split_axis=0, conca...  15.1 us
    all_to_all x2, starting transfers between devices, aggregate(): lax.all_to_all(outgoing, 'node', split_axis=0, concat_axis=0, tiled=True)  11.6 us
  transfers between devices with their start and end apart: 14, of which 8 were waited for; matrix products, arithmetic and copies ran while one was open for 22% of the time, Pallas kernels for 0%

profile of v1, /device:TPU:0, one launch (start us, length us, event | category | flops | bytes accessed | tf_op | source)
XLA Modules:
  0.0 558.8 jit_solution(2945809125494404508)
XLA Ops:
  7.2 1.5 fusion.62
  8.6 5.4 collective-permute-start.2
  17.1 2.2 gather_fusion.2
  19.3 8.0 %all-to-all-start.1 = ((bf16[16,2,8,512]{3,2,1,0:T(8,128)(2,1)}), bf16[16,2,8,512]{3,2,1,0:T(8,128)(2,1)S(1)}, u32[]{:S(2)}, u32[]{:S(2)}) async-start(bf16[16,2,8,512]{3,2,1,0:T(8,128)(2,1)} %bitcast.29), calls=%async_computation.1 | async-start | bytes 524288 | tf_op jit(solution)/shard_map/all_to_all | solution.py:78
  30.2 1.3 fusion.45
  31.9 10.0 %select_select_fusion = s32[128,32]{0,1:T(8,128)S(1)} fusion(s32[128,32]{0,1:T(8,128)S(1)} %get-tuple-element.63, s32[]{:T(128)} %bitcast.5, s32[]{:T(128)} %bitcast.6, s32[]{:T(128)} %bitcast.7, s32[]{:T(128)} %bitcast.8, s32[]{:T(128)} %bitcast.9, s32[]{:T(128)} %bitcast.10, s32[]{:T(128)} %bitcast.11, s32[]{:T(128)} %bitcast.12, s32[]{:T(128)} %bitcast.13, ...), kind=kLoop, calls=%fused_computation.100 | loop fusion | flops 139264 | bytes 32832 | tf_op jit(solution)/shard_map/jit(_take)/select_n | solution.py:42
  42.0 10.8 %gather_fusion = s32[4096,2]{1,0:T(8,128)S(1)} fusion(s32[16,2]{1,0:T(8,128)S(1)} %constant_dynamic-slice_fusion, s32[4096]{0:T(1024)S(1)} %broadcast_clamp_fusion), kind=kCustom, calls=%fused_computation | custom fusion | bytes 81920 | tf_op jit(solution)/shard_map/jit(_take)/gather | solution.py:40
  52.8 6.2 %fusion.57 = (pred[128,32]{1,0:T(8,128)(4,1)}, pred[128,32,2]{2,1,0:T(8,128)(4,1)S(1)}) fusion(s32[128,32]{1,0:T(8,128)S(1)} %copy.64, s32[128,32]{1,0:T(8,128)S(1)} %copy.63, s32[128,32,2]{2,1,0:T(8,128)S(1)} %bitcast.92, pred[128,32]{1,0:T(8,128)(4,1)} %copy.60), kind=kLoop, calls=%fused_computation.136 | loop fusion | flops 36864 | bytes 81920 | tf_op jit(solution)/shard_map/reduce_or | solution.py:45
  60.8 5.1 iota_reduce_fusion
  68.6 21.9 %scatter_custom_fusion.3 = f32[24576]{0:T(1024)S(1)} fusion(s32[4096]{0:T(1024)S(1)} %reshape.324, f32[4096]{0:T(1024)S(1)} %reshape.326, f32[]{:T(128)} %constant.212.clone.1), kind=kCustom, calls=%fused_computation.67 | custom fusion | flops 4096 | bytes 98308
  90.5 7.1 %scatter_fusion = f32[128,192]{0,1:T(8,128)S(1)} fusion(f32[128,192]{0,1:T(8,128)S(1)} %bitcast.93, s32[128]{0:T(128)S(1)} %fusion.52, f32[128]{0:T(128)S(1)} %broadcast.327), kind=kCustom, calls=%fused_computation.4 | custom fusion | flops 128 | bytes 2560 | tf_op jit(solution)/shard_map/scatter-add | solution.py:57
  98.2 3.8 collective-permute-start
  103.7 28.8 %scatter_custom_fusion.4 = f32[32768]{0:T(1024)S(1)} fusion(s32[4096]{0:T(1024)S(1)} %reshape.330, f32[4096]{0:T(1024)S(1)} %reshape.332, f32[]{:T(128)} %constant.212.clone.1), kind=kCustom, calls=%fused_computation.65 | custom fusion | flops 4096 | bytes 131076
  133.6 7.7 %all-to-all-start = ((bf16[16,2,8,512]{3,2,1,0:T(8,128)(2,1)}), bf16[16,2,8,512]{3,2,1,0:T(8,128)(2,1)S(1)}, u32[]{:S(2)}, u32[]{:S(2)}) async-start(bf16[16,2,8,512]{3,2,1,0:T(8,128)(2,1)} %bitcast.25), calls=%async_computation | async-start | bytes 524288 | tf_op jit(solution)/shard_map/all_to_all | solution.py:99
  142.9 6.8 %all-to-all-done = bf16[16,2,8,512]{3,2,1,0:T(8,128)(2,1)S(1)} async-done(((bf16[16,2,8,512]{3,2,1,0:T(8,128)(2,1)}), bf16[16,2,8,512]{3,2,1,0:T(8,128)(2,1)S(1)}, u32[]{:S(2)}, u32[]{:S(2)}) %all-to-all-start) | async-done | bytes 262176 | tf_op jit(solution)/shard_map/all_to_all | solution.py:99
  149.8 1.9 scatter_fusion.1
  151.9 1.3 fusion.68
  154.5 3.5 all-to-all-start.3
  158.1 3.8 collective-permute-start.6
  161.9 1.3 collective-permute-start.7
  163.2 3.6 all-to-all-done.3
  167.1 1.3 collective-permute-done.7
  168.4 1.5 fusion.7
  171.2 7.5 %all-to-all-start.2 = ((bf16[16,2,8,512]{3,2,1,0:T(8,128)(2,1)}), bf16[16,2,8,512]{3,2,1,0:T(8,128)(2,1)S(1)}, u32[]{:S(2)}, u32[]{:S(2)}) async-start(bf16[16,2,8,512]{3,2,1,0:T(8,128)(2,1)} %bitcast.32), calls=%async_computation.2 | async-start | bytes 524288 | tf_op jit(solution)/shard_map/all_to_all | solution.py:99
  178.9 3.8 collective-permute-start.4
  184.3 4.3 collective-permute-done.5
  188.7 3.0 all-to-all-done.2
  191.7 1.9 scatter_fusion.2
  194.2 156.3 %all-gather.5.cloned.1.call-done = f32[8192,512]{1,0:T(8,128)} async-done(((f32[512,512]{1,0:T(8,128)}), f32[8192,512]{1,0:T(8,128)}) %all-gather.5.cloned.1.call-update) | async-done | bytes 16777232 | tf_op jit(solution)/shard_map/all_gather | solution.py:113
  350.5 7.9 %reduce_sum.28 = f32[512,512]{1,0:T(8,128)S(1)} reduce(f32[16,512,512]{2,1,0:T(8,128)} %bitcast.90, f32[]{:T(128)} %constant.212.clone.1), dimensions={0}, to_apply=%region_8.9 | reduce | flops 3932160 | bytes 17825796 | tf_op jit(solution)/shard_map/reduce_sum | solution.py:113
  359.4 183.8 %all-gather.7.cloned.1.call-done = f32[8192,512]{1,0:T(8,128)} async-done(((f32[512,512]{1,0:T(8,128)}), f32[8192,512]{1,0:T(8,128)}) %all-gather.7.cloned.1.call-update) | async-done | bytes 16777232 | tf_op jit(solution)/shard_map/all_gather | solution.py:113
  543.1 7.9 %reduce_sum.29 = f32[512,512]{1,0:T(8,128)S(1)} reduce(f32[16,512,512]{2,1,0:T(8,128)} %bitcast.91, f32[]{:T(128)} %constant.212.clone.1), dimensions={0}, to_apply=%region_9.10 | reduce | flops 3932160 | bytes 17825796 | tf_op jit(solution)/shard_map/reduce_sum | solution.py:113
  (96 shorter events, 23.0 us)
Async XLA Ops:
  7.2 135.5 %copy-start = (bf16[512,512]{1,0:T(8,128)(2,1)S(1)}, bf16[512,512]{1,0:T(8,128)(2,1)}, u32[]{:S(2)}) copy-start(bf16[512,512]{1,0:T(8,128)(2,1)} %param.18) | copy-start | bytes 1572868
  8.6 133.0 %collective-permute-start.2 = (bf16[32,512]{1,0:T(8,128)(2,1)}, bf16[32,512]{1,0:T(8,128)(2,1)}, u32[]{:S(2)}, u32[]{:S(2)}) collective-permute-start(bf16[32,512]{1,0:T(8,128)(2,1)} %get-tuple-element.72), channel_id=1, source_target_pairs={{0,2},{2,4},{4,6},{6,8},{8,10},{10,12},{12,14},{14,16},{16,18},{18... | collective-permute-start | bytes 98312 | tf_op jit(solution)/shard_map/ppermute | solution.py:20
  14.1 127.6 %collective-permute-start.3 = (bf16[32,512]{1,0:T(8,128)(2,1)}, bf16[32,512]{1,0:T(8,128)(2,1)}, u32[]{:S(2)}, u32[]{:S(2)}) collective-permute-start(bf16[32,512]{1,0:T(8,128)(2,1)} %get-tuple-element.73), channel_id=1, source_target_pairs={{2,0},{4,2},{6,4},{8,6},{10,8},{12,10},{14,12},{16,14},{18,16},{20... | collective-permute-start | bytes 98312 | tf_op jit(solution)/shard_map/ppermute | solution.py:23
  17.1 10.2 %copy-start.3 = (s32[1024]{0:T(1024)}, s32[1024]{0:T(1024)S(1)}, u32[]{:S(2)}) copy-start(s32[1024]{0:T(1024)S(1)} %pad_clamp_fusion) | copy-start | bytes 12292
  19.3 114.3 %all-to-all-start.1 = ((bf16[16,2,8,512]{3,2,1,0:T(8,128)(2,1)}), bf16[16,2,8,512]{3,2,1,0:T(8,128)(2,1)S(1)}, u32[]{:S(2)}, u32[]{:S(2)}) async-start(bf16[16,2,8,512]{3,2,1,0:T(8,128)(2,1)} %bitcast.29), calls=%async_computation.1 | async-start | bytes 524288 | tf_op jit(solution)/shard_map/all_to_all | solution.py:78
  52.8 14.0 %copy-start.5 = (s32[2]{0:T(128)S(1)}, s32[2]{0:T(128)}, u32[]{:S(2)}) copy-start(s32[2]{0:T(128)} %constant.253) | copy-start | bytes 28
  59.0 38.7 %copy-start.2 = (bf16[128,512]{1,0:T(8,128)(2,1)S(1)}, bf16[128,512]{1,0:T(8,128)(2,1)}, u32[]{:S(2)}) copy-start(bf16[128,512]{1,0:T(8,128)(2,1)} %param.17) | copy-start | bytes 393220
  59.0 38.7 %copy-start.6 = (bf16[512,512]{1,0:T(8,128)(2,1)S(1)}, bf16[512,512]{1,0:T(8,128)(2,1)}, u32[]{:S(2)}) copy-start(bf16[512,512]{1,0:T(8,128)(2,1)} %param.19) | copy-start | bytes 1572868
  98.0 43.7 %copy-start.1 = (bf16[128,512]{1,0:T(8,128)(2,1)S(1)}, bf16[128,512]{1,0:T(8,128)(2,1)}, u32[]{:S(2)}) copy-start(bf16[128,512]{1,0:T(8,128)(2,1)} %param.16) | copy-start | bytes 393220
  98.2 35.3 %collective-permute-start = (bf16[32,512]{1,0:T(8,128)(2,1)S(1)}, bf16[32,512]{1,0:T(8,128)(2,1)S(1)}, u32[]{:S(2)}, u32[]{:S(2)}) collective-permute-start(bf16[32,512]{1,0:T(8,128)(2,1)S(1)} %get-tuple-element.68), channel_id=1, source_target_pairs={{0,2},{2,4},{4,6},{6,8},{8,10},{10,12},{12,14},{14,16},{16,18},{18... | collective-permute-start | bytes 98312 | tf_op jit(solution)/shard_map/ppermute | solution.py:20
  102.0 31.5 %collective-permute-start.1 = (bf16[32,512]{1,0:T(8,128)(2,1)S(1)}, bf16[32,512]{1,0:T(8,128)(2,1)S(1)}, u32[]{:S(2)}, u32[]{:S(2)}) collective-permute-start(bf16[32,512]{1,0:T(8,128)(2,1)S(1)} %get-tuple-element.69), channel_id=1, source_target_pairs={{2,0},{4,2},{6,4},{8,6},{10,8},{12,10},{14,12},{16,14},{18,16},{20... | collective-permute-start | bytes 98312 | tf_op jit(solution)/shard_map/ppermute | solution.py:23
  133.6 16.2 %all-to-all-start = ((bf16[16,2,8,512]{3,2,1,0:T(8,128)(2,1)}), bf16[16,2,8,512]{3,2,1,0:T(8,128)(2,1)S(1)}, u32[]{:S(2)}, u32[]{:S(2)}) async-start(bf16[16,2,8,512]{3,2,1,0:T(8,128)(2,1)} %bitcast.25), calls=%async_computation | async-start | bytes 524288 | tf_op jit(solution)/shard_map/all_to_all | solution.py:99
  141.2 209.3 %all-gather.5.cloned.1.call-start = ((), (), s32[]{:S(2)}) async-start(), calls=%async_computation.4 | async-start | bytes 17825792 | tf_op jit(solution)/shard_map/all_gather | solution.py:113
  149.8 3.4 copy-start.4
  154.5 12.4 %all-to-all-start.3 = ((bf16[16,2,8,512]{3,2,1,0:T(8,128)(2,1)}), bf16[16,2,8,512]{3,2,1,0:T(8,128)(2,1)S(1)}, u32[]{:S(2)}, u32[]{:S(2)}) async-start(bf16[16,2,8,512]{3,2,1,0:T(8,128)(2,1)} %bitcast.37), calls=%async_computation.3 | async-start | bytes 524288 | tf_op jit(solution)/shard_map/all_to_all | solution.py:78
  158.1 385.1 %all-gather.7.cloned.1.call-start = ((), (), s32[]{:S(2)}) async-start(), calls=%async_computation.5 | async-start | bytes 17825792 | tf_op jit(solution)/shard_map/all_gather | solution.py:113
  158.1 9.0 %collective-permute-start.6 = (bf16[32,512]{1,0:T(8,128)(2,1)S(1)}, bf16[32,512]{1,0:T(8,128)(2,1)S(1)}, u32[]{:S(2)}, u32[]{:S(2)}) collective-permute-start(bf16[32,512]{1,0:T(8,128)(2,1)S(1)} %get-tuple-element.70), channel_id=1, source_target_pairs={{0,2},{2,4},{4,6},{6,8},{8,10},{10,12},{12,14},{14,16},{16,18},{18... | collective-permute-start | bytes 98312 | tf_op jit(solution)/shard_map/ppermute | solution.py:20
  161.9 6.5 %collective-permute-start.7 = (bf16[32,512]{1,0:T(8,128)(2,1)S(1)}, bf16[32,512]{1,0:T(8,128)(2,1)S(1)}, u32[]{:S(2)}, u32[]{:S(2)}) collective-permute-start(bf16[32,512]{1,0:T(8,128)(2,1)S(1)} %get-tuple-element.71), channel_id=1, source_target_pairs={{2,0},{4,2},{6,4},{8,6},{10,8},{12,10},{14,12},{16,14},{18,16},{20... | collective-permute-start | bytes 98312 | tf_op jit(solution)/shard_map/ppermute | solution.py:23
  171.2 20.4 %all-to-all-start.2 = ((bf16[16,2,8,512]{3,2,1,0:T(8,128)(2,1)}), bf16[16,2,8,512]{3,2,1,0:T(8,128)(2,1)S(1)}, u32[]{:S(2)}, u32[]{:S(2)}) async-start(bf16[16,2,8,512]{3,2,1,0:T(8,128)(2,1)} %bitcast.32), calls=%async_computation.2 | async-start | bytes 524288 | tf_op jit(solution)/shard_map/all_to_all | solution.py:99
  178.9 5.4 collective-permute-start.4
  182.7 5.9 %collective-permute-start.5 = (bf16[32,512]{1,0:T(8,128)(2,1)S(1)}, bf16[32,512]{1,0:T(8,128)(2,1)S(1)}, u32[]{:S(2)}, u32[]{:S(2)}) collective-permute-start(bf16[32,512]{1,0:T(8,128)(2,1)S(1)} %get-tuple-element.67), channel_id=1, source_target_pairs={{2,0},{4,2},{6,4},{8,6},{10,8},{12,10},{14,12},{16,14},{18,16},{20... | collective-permute-start | bytes 98312 | tf_op jit(solution)/shard_map/ppermute | solution.py:23
Sparse Core Ops, SparseCore 0:
  153.3 197.1 all-gather.4
  353.3 189.7 all-gather.6
